TPU v7x, 32 devices: a whole 2x2x4 slice. The times are simulated.
32 devices in a mesh: slab: 8 (over z, y), patch: 4 (over x, core).
Axes of the slice: x: 2, y: 2, z: 4, core: 2. Of those that a mesh axis runs over, the one named last changes fastest.
Arguments:
- fluid_state: float32 [16, 256, 256], P('slab', 'patch'), may hold values from -6 to 6
- fluid_rhs: float32 [16, 256, 256], P('slab', 'patch'), may hold values from -24 to 24
- element_scale: float32 [16, 256], P('slab', 'patch'), may hold values from 1 to 4
- element_matrix: bfloat16 [256, 256], replicated
- couple_x: bfloat16 [256, 256], replicated, may hold values from -0.09375 to 0.09375
- couple_y: bfloat16 [256, 256], replicated, may hold values from -0.09375 to 0.09375
- block_inverse: bfloat16 [256, 256], replicated
- traction_map: bfloat16 [3, 256], replicated, may hold values from -0.375 to 0.375
- slot_elem: int32 [8, 4, 1024], P('slab', 'patch'), may hold values from 0 to 127
- slot_point: int32 [8, 4, 1024], P('slab', 'patch'), may hold values from 0 to 8191
- slot_count: int32 [8, 4, 4], P('slab', 'patch'), may hold values from 0 to 256, as said below
- displacement: float32 [3, 256, 128], P(None, 'patch'), may hold values from -6 to 6
- stiffness: float32 [256, 128], P('patch'), may hold values from 0.03 to 0.3
Outputs:
- fluid_out: float32 [16, 256, 256], P('slab', 'patch')
- displacement_new: float32 [3, 256, 128], P(None, 'patch')
- wall_motion: float32 [3, 8, 4, 1024], P(None, 'slab', 'patch')
Inputs may be any that keep to these rules, and one draw needn't show every extreme that they name: For every block and owner only the first slot_count slots of that owner's 256 slots are live; the count 256 is reached for some block and owner in every draw.
All inputs are finite; a program needn't handle non-finite values.
Results may differ from a plain program's by a relative error of at most 0.0049.
Values may be sent and summed in bfloat16 or wider, within the bound.
A program may use at most 128 MiB of HBM per device.

v0:
```python
import jax
import jax.numpy as jnp
from jax import lax
from jax.sharding import PartitionSpec as P

SWEEPS = 3


def with_halo(cells, sides, width):
    for axis, dim in sides:
        count = lax.axis_size(axis)
        ends = count - 1
        head = lax.slice_in_dim(cells, 0, width, axis=dim)
        tail = lax.slice_in_dim(cells, cells.shape[dim] - width, cells.shape[dim], axis=dim)
        cells = jnp.concatenate(
            [
                lax.ppermute(tail, axis, [(i, (i + 1) % count) for i in range(ends)]),
                cells,
                lax.ppermute(head, axis, [((i + 1) % count, i) for i in range(ends)]),
            ],
            axis=dim,
        )
    return cells


def element_apply(rounded, scale, element_matrix, couple_x, couple_y):
    padded = with_halo(rounded, (("slab", 0), ("patch", 1)), 1)
    along_x = (padded[:-2, 1:-1].astype(jnp.float32) + padded[2:, 1:-1].astype(jnp.float32)).astype(
        jnp.bfloat16
    )
    along_y = (padded[1:-1, :-2].astype(jnp.float32) + padded[1:-1, 2:].astype(jnp.float32)).astype(
        jnp.bfloat16
    )
    width = rounded.shape[2]
    own = jnp.dot(rounded.reshape(-1, width), element_matrix, preferred_element_type=jnp.float32)
    side_x = jnp.dot(along_x.reshape(-1, width), couple_x, preferred_element_type=jnp.float32)
    side_y = jnp.dot(along_y.reshape(-1, width), couple_y, preferred_element_type=jnp.float32)
    return (
        scale[:, :, None] * own.reshape(rounded.shape)
        - side_x.reshape(rounded.shape)
        - side_y.reshape(rounded.shape)
    )


def laplace_net(field):
    edged = with_halo(field.astype(jnp.bfloat16), (("patch", 1),), 1).astype(field.dtype)
    edged = jnp.pad(edged, ((0, 0), (0, 0), (1, 1)))
    return 4.0 * field - (
        edged[:, 2:, 1:-1] + edged[:, :-2, 1:-1] + edged[:, 1:-1, 2:] + edged[:, 1:-1, :-2]
    )


def shards(
    fluid_state,
    fluid_rhs,
    element_scale,
    element_matrix,
    couple_x,
    couple_y,
    block_inverse,
    traction_map,
    slot_elem,
    slot_point,
    slot_count,
    displacement,
    stiffness,
):
    width = fluid_state.shape[2]
    state = fluid_state
    for sweep in range(SWEEPS):
        rounded = state.astype(jnp.bfloat16)
        applied = element_apply(rounded, element_scale, element_matrix, couple_x, couple_y)
        residue = (fluid_rhs - applied).astype(jnp.bfloat16)
        update = jnp.dot(
            residue.reshape(-1, width), block_inverse, preferred_element_type=jnp.float32
        ).reshape(state.shape)
        state = state + update / element_scale[:, :, None]
    final = state.astype(jnp.bfloat16)
    owners = lax.axis_size("patch")
    capacity = slot_elem.shape[2] // owners
    net_rows = displacement.shape[1]
    net_cols = displacement.shape[2]
    cells = net_rows * net_cols
    rows = jnp.take(final.reshape(-1, width), slot_elem.reshape(-1), axis=0).reshape(
        owners, capacity, width
    )
    pull = jnp.einsum("cd,kqd->kcq", traction_map, rows, preferred_element_type=jnp.float32)
    limits = slot_count.reshape(owners)
    live = (lax.broadcasted_iota(jnp.int32, (owners, capacity), 1) < limits[:, None]).astype(
        jnp.float32
    )
    pull = pull * live[:, None, :]
    points = slot_point.reshape(owners, capacity)
    owner_ids = lax.broadcasted_iota(jnp.int32, (owners, capacity), 0)
    got_pull, got_points = (
        lax.all_to_all(pull, "patch", split_axis=0, concat_axis=0, tiled=True),
        lax.all_to_all(points, "patch", split_axis=0, concat_axis=0, tiled=True),
    )
    local = jnp.zeros((3, cells), jnp.float32)
    local = local.at[:, got_points.reshape(-1)].add(got_pull.transpose(1, 0, 2).reshape(3, -1))
    loads = lax.psum(local, "slab")
    loads = loads.reshape(3, net_rows, net_cols)
    bend = laplace_net(displacement)
    stiff_term = stiffness[None] * (laplace_net(bend) + 4.0 * bend)
    displacement_new = displacement + (loads - stiff_term) / (36.0 * stiffness[None])
    flat_net = displacement_new.reshape(3, -1)
    whole = lax.all_gather(flat_net, "patch", axis=1, tiled=True)
    picked = whole[:, (owner_ids * cells + points).reshape(-1)]
    wall_motion = (picked * live.reshape(1, -1)).reshape(3, 1, 1, owners * capacity)
    return (state, displacement_new, wall_motion)


def solution(mesh):
    return jax.shard_map(
        shards,
        mesh=mesh,
        in_specs=(
            P("slab", "patch", None),
            P("slab", "patch", None),
            P("slab", "patch"),
            P(),
            P(),
            P(),
            P(),
            P(),
            P("slab", "patch", None),
            P("slab", "patch", None),
            P("slab", "patch", None),
            P(None, "patch", None),
            P("patch", None),
        ),
        out_specs=(
            P("slab", "patch", None),
            P(None, "patch", None),
            P(None, "slab", "patch", None),
        ),
        check_vma=False,
    )
```

profile of v0, /device:TPU:0, one launch (start us, length us, event | category | flops | bytes accessed | tf_op | source)
XLA Modules:
  0.0 299.1 jit_solution(18253544204650045127)
XLA Ops:
  8.3 1.3 collective-permute-start.1
  9.6 5.5 %collective-permute-start = (bf16[1,64,256]{2,1,0:T(8,128)(2,1)S(1)}, bf16[1,64,256]{2,1,0:T(8,128)(2,1)S(1)}, u32[]{:S(2)}, u32[]{:S(2)}) collective-permute-start(bf16[1,64,256]{2,1,0:T(8,128)(2,1)S(1)} %get-tuple-element.24), channel_id=1, source_target_pairs={{0,4},{4,8},{8,12},{12,16},{16,20},{20,24},{24,28},{1,5},{5,9},{9,... | collective-permute-start | bytes 98312 | tf_op jit(solution)/shard_map/ppermute | solution.py:17
  15.1 3.3 %all-to-all-start = ((s32[4,1,256]{2,1,0:T(1,128)}), s32[4,1,256]{2,1,0:T(1,128)S(1)}, u32[]{:S(2)}, u32[]{:S(2)}) async-start(s32[4,1,256]{2,1,0:T(1,128)} %bitcast.90), calls=%async_computation | async-start | bytes 8192 | tf_op jit(solution)/shard_map/all_to_all | solution.py:97
  19.3 1.3 collective-permute-start.13
  20.6 3.0 %collective-permute-start.12 = (bf16[3,1,128]{2,1,0:T(2,128)(2,1)S(1)}, bf16[3,1,128]{2,1,0:T(2,128)(2,1)S(1)}, u32[]{:S(2)}, u32[]{:S(2)}) collective-permute-start(bf16[3,1,128]{2,1,0:T(2,128)(2,1)S(1)} %get-tuple-element.28), channel_id=1, source_target_pairs={{0,1},{1,2},{2,3},{4,5},{5,6},{6,7},{8,9},{9,10},{10,11},{12,13},{... | collective-permute-start | bytes 2312 | tf_op jit(solution)/shard_map/ppermute | solution.py:17
  24.9 1.3 reduce.3
  27.8 1.1 convolution_multiply_fusion.2
  30.7 1.3 collective-permute-start.15
  32.0 4.3 %collective-permute-start.14 = (bf16[3,1,128]{2,1,0:T(2,128)(2,1)S(1)}, bf16[3,1,128]{2,1,0:T(2,128)(2,1)S(1)}, u32[]{:S(2)}, u32[]{:S(2)}) collective-permute-start(bf16[3,1,128]{2,1,0:T(2,128)(2,1)S(1)} %get-tuple-element.26), channel_id=1, source_target_pairs={{0,1},{1,2},{2,3},{4,5},{5,6},{6,7},{8,9},{9,10},{10,11},{12,13},{... | collective-permute-start | bytes 2312 | tf_op jit(solution)/shard_map/ppermute | solution.py:17
  36.3 1.3 collective-permute-start.3
  37.6 4.3 %collective-permute-start.2 = (bf16[4,1,256]{2,1,0:T(2,128)(2,1)S(1)}, bf16[4,1,256]{2,1,0:T(2,128)(2,1)S(1)}, u32[]{:S(2)}, u32[]{:S(2)}) collective-permute-start(bf16[4,1,256]{2,1,0:T(2,128)(2,1)S(1)} %get-tuple-element.18), channel_id=1, source_target_pairs={{0,1},{1,2},{2,3},{4,5},{5,6},{6,7},{8,9},{9,10},{10,11},{12,13},{... | collective-permute-start | bytes 6152 | tf_op jit(solution)/shard_map/ppermute | solution.py:17
  41.9 1.1 convolution_subtract_fusion.5
  43.0 1.3 fusion.77
  44.3 1.3 collective-permute-start.5
  45.6 5.4 %collective-permute-start.4 = (bf16[1,64,256]{2,1,0:T(8,128)(2,1)S(1)}, bf16[1,64,256]{2,1,0:T(8,128)(2,1)S(1)}, u32[]{:S(2)}, u32[]{:S(2)}) collective-permute-start(bf16[1,64,256]{2,1,0:T(8,128)(2,1)S(1)} %get-tuple-element.22), channel_id=1, source_target_pairs={{0,4},{4,8},{8,12},{12,16},{16,20},{20,24},{24,28},{1,5},{5,9},{9,... | collective-permute-start | bytes 98312 | tf_op jit(solution)/shard_map/ppermute | solution.py:17
  51.1 1.1 convolution_multiply_fusion.1
  52.6 1.3 collective-permute-start.7
  53.9 3.5 %collective-permute-start.6 = (bf16[4,1,256]{2,1,0:T(2,128)(2,1)S(1)}, bf16[4,1,256]{2,1,0:T(2,128)(2,1)S(1)}, u32[]{:S(2)}, u32[]{:S(2)}) collective-permute-start(bf16[4,1,256]{2,1,0:T(2,128)(2,1)S(1)} %get-tuple-element.16), channel_id=1, source_target_pairs={{0,1},{1,2},{2,3},{4,5},{5,6},{6,7},{8,9},{9,10},{10,11},{12,13},{... | collective-permute-start | bytes 6152 | tf_op jit(solution)/shard_map/ppermute | solution.py:17
  58.6 1.3 collective-permute-start.9
  59.9 5.2 %collective-permute-start.8 = (bf16[1,64,256]{2,1,0:T(8,128)(2,1)S(1)}, bf16[1,64,256]{2,1,0:T(8,128)(2,1)S(1)}, u32[]{:S(2)}, u32[]{:S(2)}) collective-permute-start(bf16[1,64,256]{2,1,0:T(8,128)(2,1)S(1)} %get-tuple-element.20), channel_id=1, source_target_pairs={{0,4},{4,8},{8,12},{12,16},{16,20},{20,24},{24,28},{1,5},{5,9},{9,... | collective-permute-start | bytes 98312 | tf_op jit(solution)/shard_map/ppermute | solution.py:17
  65.3 1.4 collective-permute-done.8
  66.7 1.3 collective-permute-start.11
  68.0 4.5 %collective-permute-start.10 = (bf16[4,1,256]{2,1,0:T(2,128)(2,1)S(1)}, bf16[4,1,256]{2,1,0:T(2,128)(2,1)S(1)}, u32[]{:S(2)}, u32[]{:S(2)}) collective-permute-start(bf16[4,1,256]{2,1,0:T(2,128)(2,1)S(1)} %get-tuple-element.14), channel_id=1, source_target_pairs={{0,1},{1,2},{2,3},{4,5},{5,6},{6,7},{8,9},{9,10},{10,11},{12,13},{... | collective-permute-start | bytes 6152 | tf_op jit(solution)/shard_map/ppermute | solution.py:17
  74.3 3.9 %gather_fusion = bf16[1024,256]{1,0:T(8,128)(2,1)S(1)} fusion(bf16[128,256]{1,0:T(8,128)(2,1)S(1)} %bitcast.84, s32[1024]{0:T(1024)S(1)} %broadcast_clamp_fusion.1), kind=kCustom, calls=%fused_computation | custom fusion | bytes 1052672 | tf_op jit(solution)/shard_map/jit(_take)/gather | solution.py:84
  79.2 6.5 %all-to-all-start.1 = ((f32[4,3,256]{2,1,0:T(4,128)}), f32[4,3,256]{2,1,0:T(4,128)S(1)}, u32[]{:S(2)}, u32[]{:S(2)}) async-start(f32[4,3,256]{2,1,0:T(4,128)} %fusion.11), calls=%async_computation.1 | async-start | bytes 32768 | tf_op jit(solution)/shard_map/all_to_all | solution.py:96
  85.7 3.8 %all-to-all-done.1 = f32[4,3,256]{2,1,0:T(4,128)S(1)} async-done(((f32[4,3,256]{2,1,0:T(4,128)}), f32[4,3,256]{2,1,0:T(4,128)S(1)}, u32[]{:S(2)}, u32[]{:S(2)}) %all-to-all-start.1) | async-done | bytes 12320 | tf_op jit(solution)/shard_map/all_to_all | solution.py:96
  89.8 8.2 %scatter_custom_fusion = f32[3,8192]{0,1:T(8,128)} fusion(s32[1024]{0:T(1024)S(1)} %bitcast.95, f32[1024,3]{1,0:T(8,128)S(1)} %copy.23, f32[]{:T(128)} %constant.9.clone.1), kind=kCustom, calls=%fused_computation.3 | custom fusion | flops 3072 | bytes 98308 | tf_op jit(solution)/shard_map/scatter-add | solution.py:100
  98.0 3.5 %copy.24 = f32[3,64,128]{2,1,0:T(8,128)} copy(f32[3,64,128]{0,2,1:T(8,128)} %bitcast.86) | data formatting | bytes 196608 | tf_op jit(solution)/shard_map/reshape | solution.py:102
  101.6 73.6 %all-reduce.4.cloned.1.call-done = f32[3,64,128]{2,1,0:T(8,128)} async-done(((f32[3,64,128]{2,1,0:T(8,128)}), f32[3,64,128]{2,1,0:T(8,128)}) %all-reduce.4.cloned.1.call-update) | async-done | bytes 98320 | tf_op jit(solution)/shard_map/psum | solution.py:101
  176.2 2.6 copy.25
  178.8 103.9 %all_gather.3 = f32[3,32768]{0,1:T(8,128)} all-gather(f32[3,8192]{0,1:T(8,128)} %bitcast.85), channel_id=1, replica_groups=mesh['slab'=8,'patch'=4] {'patch'}, dimensions={1}, use_global_device_ids=true | all-gather | bytes 491520 | tf_op jit(solution)/shard_map/all_gather | solution.py:107
  282.7 8.6 %gather_fusion.1 = f32[1024,3]{1,0:T(8,128)S(1)} fusion(f32[3,32768]{0,1:T(8,128)} %all_gather.3, s32[1024]{0:T(1024)S(1)} %broadcast_clamp_fusion), kind=kCustom, calls=%fused_computation.1 | custom fusion | bytes 28672 | tf_op jit(solution)/shard_map/gather | solution.py:108
  (74 shorter events, 13.3 us)
Async XLA Ops:
  7.2 35.8 %copy-start = (bf16[256,256]{1,0:T(8,128)(2,1)S(1)}, bf16[256,256]{1,0:T(8,128)(2,1)}, u32[]{:S(2)}) copy-start(bf16[256,256]{1,0:T(8,128)(2,1)} %param.19) | copy-start | bytes 393220
  7.2 51.1 %copy-start.6 = (f32[2,64]{1,0:T(2,128)S(1)}, f32[2,64]{1,0:T(2,128)}, u32[]{:S(2)}) copy-start(f32[2,64]{1,0:T(2,128)} %param.15) | copy-start | bytes 1540
  7.2 57.9 %copy-start.1 = (bf16[256,256]{1,0:T(8,128)(2,1)S(1)}, bf16[256,256]{1,0:T(8,128)(2,1)}, u32[]{:S(2)}) copy-start(bf16[256,256]{1,0:T(8,128)(2,1)} %param.16) | copy-start | bytes 393220
  7.2 50.3 %copy-start.2 = (bf16[256,256]{1,0:T(8,128)(2,1)S(1)}, bf16[256,256]{1,0:T(8,128)(2,1)}, u32[]{:S(2)}) copy-start(bf16[256,256]{1,0:T(8,128)(2,1)} %param.17) | copy-start | bytes 393220
  7.2 51.1 %copy-start.7 = (f32[2,64,256]{2,1,0:T(8,128)S(1)}, f32[2,64,256]{2,1,0:T(8,128)}, u32[]{:S(2)}) copy-start(f32[2,64,256]{2,1,0:T(8,128)} %param.14) | copy-start | bytes 393220
  7.2 51.1 %copy-start.8 = (bf16[256,256]{1,0:T(8,128)(2,1)S(1)}, bf16[256,256]{1,0:T(8,128)(2,1)}, u32[]{:S(2)}) copy-start(bf16[256,256]{1,0:T(8,128)(2,1)} %param.18) | copy-start | bytes 393220
  8.3 28.0 %collective-permute-start.1 = (bf16[1,64,256]{2,1,0:T(8,128)(2,1)S(1)}, bf16[1,64,256]{2,1,0:T(8,128)(2,1)S(1)}, u32[]{:S(2)}, u32[]{:S(2)}) collective-permute-start(bf16[1,64,256]{2,1,0:T(8,128)(2,1)S(1)} %get-tuple-element.25), channel_id=1, source_target_pairs={{4,0},{8,4},{12,8},{16,12},{20,16},{24,20},{28,24},{5,1},{9,5},{13... | collective-permute-start | bytes 98312 | tf_op jit(solution)/shard_map/ppermute | solution.py:19
  9.6 26.7 %collective-permute-start = (bf16[1,64,256]{2,1,0:T(8,128)(2,1)S(1)}, bf16[1,64,256]{2,1,0:T(8,128)(2,1)S(1)}, u32[]{:S(2)}, u32[]{:S(2)}) collective-permute-start(bf16[1,64,256]{2,1,0:T(8,128)(2,1)S(1)} %get-tuple-element.24), channel_id=1, source_target_pairs={{0,4},{4,8},{8,12},{12,16},{16,20},{20,24},{24,28},{1,5},{5,9},{9,... | collective-permute-start | bytes 98312 | tf_op jit(solution)/shard_map/ppermute | solution.py:17
  15.1 64.1 %all-to-all-start = ((s32[4,1,256]{2,1,0:T(1,128)}), s32[4,1,256]{2,1,0:T(1,128)S(1)}, u32[]{:S(2)}, u32[]{:S(2)}) async-start(s32[4,1,256]{2,1,0:T(1,128)} %bitcast.90), calls=%async_computation | async-start | bytes 8192 | tf_op jit(solution)/shard_map/all_to_all | solution.py:97
  19.3 10.3 %collective-permute-start.13 = (bf16[3,1,128]{2,1,0:T(2,128)(2,1)S(1)}, bf16[3,1,128]{2,1,0:T(2,128)(2,1)S(1)}, u32[]{:S(2)}, u32[]{:S(2)}) collective-permute-start(bf16[3,1,128]{2,1,0:T(2,128)(2,1)S(1)} %get-tuple-element.29), channel_id=1, source_target_pairs={{1,0},{2,1},{3,2},{5,4},{6,5},{7,6},{9,8},{10,9},{11,10},{13,12},{... | collective-permute-start | bytes 2312 | tf_op jit(solution)/shard_map/ppermute | solution.py:19
  20.6 9.0 %collective-permute-start.12 = (bf16[3,1,128]{2,1,0:T(2,128)(2,1)S(1)}, bf16[3,1,128]{2,1,0:T(2,128)(2,1)S(1)}, u32[]{:S(2)}, u32[]{:S(2)}) collective-permute-start(bf16[3,1,128]{2,1,0:T(2,128)(2,1)S(1)} %get-tuple-element.28), channel_id=1, source_target_pairs={{0,1},{1,2},{2,3},{4,5},{5,6},{6,7},{8,9},{9,10},{10,11},{12,13},{... | collective-permute-start | bytes 2312 | tf_op jit(solution)/shard_map/ppermute | solution.py:17
  30.7 70.8 %collective-permute-start.15 = (bf16[3,1,128]{2,1,0:T(2,128)(2,1)S(1)}, bf16[3,1,128]{2,1,0:T(2,128)(2,1)S(1)}, u32[]{:S(2)}, u32[]{:S(2)}) collective-permute-start(bf16[3,1,128]{2,1,0:T(2,128)(2,1)S(1)} %get-tuple-element.27), channel_id=1, source_target_pairs={{1,0},{2,1},{3,2},{5,4},{6,5},{7,6},{9,8},{10,9},{11,10},{13,12},{... | collective-permute-start | bytes 2312 | tf_op jit(solution)/shard_map/ppermute | solution.py:19
  32.0 69.6 %collective-permute-start.14 = (bf16[3,1,128]{2,1,0:T(2,128)(2,1)S(1)}, bf16[3,1,128]{2,1,0:T(2,128)(2,1)S(1)}, u32[]{:S(2)}, u32[]{:S(2)}) collective-permute-start(bf16[3,1,128]{2,1,0:T(2,128)(2,1)S(1)} %get-tuple-element.26), channel_id=1, source_target_pairs={{0,1},{1,2},{2,3},{4,5},{5,6},{6,7},{8,9},{9,10},{10,11},{12,13},{... | collective-permute-start | bytes 2312 | tf_op jit(solution)/shard_map/ppermute | solution.py:17
  36.3 6.7 %collective-permute-start.3 = (bf16[4,1,256]{2,1,0:T(2,128)(2,1)S(1)}, bf16[4,1,256]{2,1,0:T(2,128)(2,1)S(1)}, u32[]{:S(2)}, u32[]{:S(2)}) collective-permute-start(bf16[4,1,256]{2,1,0:T(2,128)(2,1)S(1)} %get-tuple-element.19), channel_id=1, source_target_pairs={{1,0},{2,1},{3,2},{5,4},{6,5},{7,6},{9,8},{10,9},{11,10},{13,12},{... | collective-permute-start | bytes 6152 | tf_op jit(solution)/shard_map/ppermute | solution.py:19
  37.6 5.4 %collective-permute-start.2 = (bf16[4,1,256]{2,1,0:T(2,128)(2,1)S(1)}, bf16[4,1,256]{2,1,0:T(2,128)(2,1)S(1)}, u32[]{:S(2)}, u32[]{:S(2)}) collective-permute-start(bf16[4,1,256]{2,1,0:T(2,128)(2,1)S(1)} %get-tuple-element.18), channel_id=1, source_target_pairs={{0,1},{1,2},{2,3},{4,5},{5,6},{6,7},{8,9},{9,10},{10,11},{12,13},{... | collective-permute-start | bytes 6152 | tf_op jit(solution)/shard_map/ppermute | solution.py:17
  44.3 7.8 %collective-permute-start.5 = (bf16[1,64,256]{2,1,0:T(8,128)(2,1)S(1)}, bf16[1,64,256]{2,1,0:T(8,128)(2,1)S(1)}, u32[]{:S(2)}, u32[]{:S(2)}) collective-permute-start(bf16[1,64,256]{2,1,0:T(8,128)(2,1)S(1)} %get-tuple-element.23), channel_id=1, source_target_pairs={{4,0},{8,4},{12,8},{16,12},{20,16},{24,20},{28,24},{5,1},{9,5},{13... | collective-permute-start | bytes 98312 | tf_op jit(solution)/shard_map/ppermute | solution.py:19
  45.6 7.0 %collective-permute-start.4 = (bf16[1,64,256]{2,1,0:T(8,128)(2,1)S(1)}, bf16[1,64,256]{2,1,0:T(8,128)(2,1)S(1)}, u32[]{:S(2)}, u32[]{:S(2)}) collective-permute-start(bf16[1,64,256]{2,1,0:T(8,128)(2,1)S(1)} %get-tuple-element.22), channel_id=1, source_target_pairs={{0,4},{4,8},{8,12},{12,16},{16,20},{20,24},{24,28},{1,5},{5,9},{9,... | collective-permute-start | bytes 98312 | tf_op jit(solution)/shard_map/ppermute | solution.py:17
  52.6 5.0 %collective-permute-start.7 = (bf16[4,1,256]{2,1,0:T(2,128)(2,1)S(1)}, bf16[4,1,256]{2,1,0:T(2,128)(2,1)S(1)}, u32[]{:S(2)}, u32[]{:S(2)}) collective-permute-start(bf16[4,1,256]{2,1,0:T(2,128)(2,1)S(1)} %get-tuple-element.17), channel_id=1, source_target_pairs={{1,0},{2,1},{3,2},{5,4},{6,5},{7,6},{9,8},{10,9},{11,10},{13,12},{... | collective-permute-start | bytes 6152 | tf_op jit(solution)/shard_map/ppermute | solution.py:19
  53.9 4.3 %collective-permute-start.6 = (bf16[4,1,256]{2,1,0:T(2,128)(2,1)S(1)}, bf16[4,1,256]{2,1,0:T(2,128)(2,1)S(1)}, u32[]{:S(2)}, u32[]{:S(2)}) collective-permute-start(bf16[4,1,256]{2,1,0:T(2,128)(2,1)S(1)} %get-tuple-element.16), channel_id=1, source_target_pairs={{0,1},{1,2},{2,3},{4,5},{5,6},{6,7},{8,9},{9,10},{10,11},{12,13},{... | collective-permute-start | bytes 6152 | tf_op jit(solution)/shard_map/ppermute | solution.py:17
  57.6 20.6 %copy-start.9 = (bf16[3,256]{1,0:T(4,128)(2,1)S(1)}, bf16[3,256]{1,0:T(4,128)(2,1)}, u32[]{:S(2)}) copy-start(bf16[3,256]{1,0:T(4,128)(2,1)} %param.20) | copy-start | bytes 4612
  58.6 6.7 %collective-permute-start.9 = (bf16[1,64,256]{2,1,0:T(8,128)(2,1)S(1)}, bf16[1,64,256]{2,1,0:T(8,128)(2,1)S(1)}, u32[]{:S(2)}, u32[]{:S(2)}) collective-permute-start(bf16[1,64,256]{2,1,0:T(8,128)(2,1)S(1)} %get-tuple-element.21), channel_id=1, source_target_pairs={{4,0},{8,4},{12,8},{16,12},{20,16},{24,20},{28,24},{5,1},{9,5},{13... | collective-permute-start | bytes 98312 | tf_op jit(solution)/shard_map/ppermute | solution.py:19
  59.9 6.8 %collective-permute-start.8 = (bf16[1,64,256]{2,1,0:T(8,128)(2,1)S(1)}, bf16[1,64,256]{2,1,0:T(8,128)(2,1)S(1)}, u32[]{:S(2)}, u32[]{:S(2)}) collective-permute-start(bf16[1,64,256]{2,1,0:T(8,128)(2,1)S(1)} %get-tuple-element.20), channel_id=1, source_target_pairs={{0,4},{4,8},{8,12},{12,16},{16,20},{20,24},{24,28},{1,5},{5,9},{9,... | collective-permute-start | bytes 98312 | tf_op jit(solution)/shard_map/ppermute | solution.py:17
  66.7 6.0 %collective-permute-start.11 = (bf16[4,1,256]{2,1,0:T(2,128)(2,1)S(1)}, bf16[4,1,256]{2,1,0:T(2,128)(2,1)S(1)}, u32[]{:S(2)}, u32[]{:S(2)}) collective-permute-start(bf16[4,1,256]{2,1,0:T(2,128)(2,1)S(1)} %get-tuple-element.15), channel_id=1, source_target_pairs={{1,0},{2,1},{3,2},{5,4},{6,5},{7,6},{9,8},{10,9},{11,10},{13,12},{... | collective-permute-start | bytes 6152 | tf_op jit(solution)/shard_map/ppermute | solution.py:19
  68.0 5.4 %collective-permute-start.10 = (bf16[4,1,256]{2,1,0:T(2,128)(2,1)S(1)}, bf16[4,1,256]{2,1,0:T(2,128)(2,1)S(1)}, u32[]{:S(2)}, u32[]{:S(2)}) collective-permute-start(bf16[4,1,256]{2,1,0:T(2,128)(2,1)S(1)} %get-tuple-element.14), channel_id=1, source_target_pairs={{0,1},{1,2},{2,3},{4,5},{5,6},{6,7},{8,9},{9,10},{10,11},{12,13},{... | collective-permute-start | bytes 6152 | tf_op jit(solution)/shard_map/ppermute | solution.py:17
  79.2 10.4 %all-to-all-start.1 = ((f32[4,3,256]{2,1,0:T(4,128)}), f32[4,3,256]{2,1,0:T(4,128)S(1)}, u32[]{:S(2)}, u32[]{:S(2)}) async-start(f32[4,3,256]{2,1,0:T(4,128)} %fusion.11), calls=%async_computation.1 | async-start | bytes 32768 | tf_op jit(solution)/shard_map/all_to_all | solution.py:96
  85.7 89.5 %all-reduce.4.cloned.1.call-start = ((), (), s32[]{:S(2)}) async-start(), calls=%async_computation.2 | async-start | bytes 196608 | tf_op jit(solution)/shard_map/psum | solution.py:101
  89.8 85.4 %copy-start.3 = (f32[3,64,128]{2,1,0:T(8,128)S(1)}, f32[3,64,128]{2,1,0:T(8,128)}, u32[]{:S(2)}) copy-start(f32[3,64,128]{2,1,0:T(8,128)} %param.24) | copy-start | bytes 294916
  89.8 85.4 %copy-start.5 = (f32[64,128]{1,0:T(8,128)S(1)}, f32[64,128]{1,0:T(8,128)}, u32[]{:S(2)}) copy-start(f32[64,128]{1,0:T(8,128)} %param.25) | copy-start | bytes 98308
  176.2 106.5 %copy-start.4 = (f32[3,64,128]{2,1,0:T(8,128)}, f32[3,64,128]{2,1,0:T(8,128)S(1)}, u32[]{:S(2)}) copy-start(f32[3,64,128]{2,1,0:T(8,128)S(1)} %fusion.33) | copy-start | bytes 294916
Sparse Core Ops, SparseCore 0:
  101.6 73.4 all-reduce.3
where the time goes:
time: 300 us; the launch traced here: 299 us
  blocking collectives  104 us (35%)
  waiting for transfers between devices  80.6 us (27%)
  starting transfers between devices  55.9 us (19%)
  local copies, waits for them, and re-layouts  20.3 us (7%)
  other arithmetic  16.7 us (6%)
  between operations  14.5 us (5%)
  matrix products  7.25 us (2%)
    all_gather x1, blocking collectives, shards(): whole = lax.all_gather(flat_net, 'patch', axis=1, tiled=True)  104 us
    psum x1, waiting for transfers between devices, shards(): loads = lax.psum(local, 'slab')  73.6 us
    ppermute x8, starting transfers between devices, with_halo(): lax.ppermute(tail, axis, [(i, (i + 1) % count) for i in range(ends)])  35.8 us
    ppermute x8, starting transfers between devices, with_halo(): lax.ppermute(head, axis, [((i + 1) % count, i) for i in range(ends)])  10.3 us
    gather x1, local copies, waits for them, and re-layouts, shards(): picked = whole[:, (owner_ids * cells + points).reshape(-1)]  8.57 us
    scatter-add x1, other arithmetic, shards(): local.at[:, got_points.reshape(-1)]  8.21 us
    all_to_all x1, starting transfers between devices, shards(): lax.all_to_all(pull, 'patch', split_axis=0, concat_axis=0, tiled=True)  6.5 us
  transfers between devices with their start and end apart: 19, of which 6 were waited for; matrix products, arithmetic and copies ran while one was open for 10% of the time, Pallas kernels for 0%

commit v1 on v0

--- a/solution.py
+++ b/solution.py
@@ -4,6 +4,11 @@
 from jax.sharding import PartitionSpec as P
 
 SWEEPS = 3
+
+
+def move_the_spans(array_in, dev_axis):
+    taken_in = jnp.sum(jax.lax.all_gather(array_in, dev_axis), axis=0)
+    return taken_in
 
 
 def with_halo(cells, sides, width):
@@ -98,7 +103,7 @@
     )
     local = jnp.zeros((3, cells), jnp.float32)
     local = local.at[:, got_points.reshape(-1)].add(got_pull.transpose(1, 0, 2).reshape(3, -1))
-    loads = lax.psum(local, "slab")
+    loads = move_the_spans(local, "slab")
     loads = loads.reshape(3, net_rows, net_cols)
     bend = laplace_net(displacement)
     stiff_term = stiffness[None] * (laplace_net(bend) + 4.0 * bend)

time: 300 us -> 251 us (0.84)
  waiting for transfers between devices: 80.6 us -> 7.76 us
  blocking collectives: 104 us -> 136 us
  between operations: 14.5 us -> 1.15 us
  local copies, waits for them, and re-layouts: 20.3 us -> 25.2 us
    psum x1 -> x0, waiting for transfers between devices: 73.6 us -> none  [shards(): loads = lax.psum(local, 'slab')]
    all_gather x0 -> x1, blocking collectives: none -> 36.5 us  [move_the_spans(): taken_in = jnp.sum(jax.lax.all_gather(array_in, dev_axis), axis=0)]
    unnamed x25 -> x27, local copies, waits for them, and re-layouts: 1.45 us -> 6.95 us
    all_gather x1, blocking collectives: 104 us -> 99.3 us  [shards(): whole = lax.all_gather(flat_net, 'patch', axis=1, tiled=True)]
  transfers between devices with their start and end apart: 19 -> 18, of which waited for: 6 -> 6; matrix products, arithmetic and copies ran while one was open for 10% -> 7% of each run, Pallas kernels for 0% -> 0%
where the time goes in v1:
time: 251 us; the launch traced here: 250 us
  blocking collectives  136 us (54%)
  starting transfers between devices  56.3 us (22%)
  local copies, waits for them, and re-layouts  25.2 us (10%)
  other arithmetic  16 us (6%)
  waiting for transfers between devices  7.76 us (3%)
  matrix products  7.25 us (3%)
    all_gather x1, blocking collectives, shards(): whole = lax.all_gather(flat_net, 'patch', axis=1, tiled=True)  99.3 us
    all_gather x1, blocking collectives, move_the_spans(): taken_in = jnp.sum(jax.lax.all_gather(array_in, dev_axis), axis=0)  36.5 us
    ppermute x8, starting transfers between devices, with_halo(): lax.ppermute(tail, axis, [(i, (i + 1) % count) for i in range(ends)])  36.2 us
    ppermute x8, starting transfers between devices, with_halo(): lax.ppermute(head, axis, [((i + 1) % count, i) for i in range(ends)])  10.3 us
    gather x1, local copies, waits for them, and re-layouts, shards(): picked = whole[:, (owner_ids * cells + points).reshape(-1)]  8.57 us
    scatter-add x1, other arithmetic, shards(): local.at[:, got_points.reshape(-1)]  8.2 us
    unnamed x27, local copies, waits for them, and re-layouts  6.95 us
    all_to_all x1, starting transfers between devices, shards(): lax.all_to_all(pull, 'patch', split_axis=0, concat_axis=0, tiled=True)  6.5 us
  transfers between devices with their start and end apart: 18, of which 6 were waited for; matrix products, arithmetic and copies ran while one was open for 7% of the time, Pallas kernels for 0%

profile of v1, /device:TPU:0, one launch (start us, length us, event | category | flops | bytes accessed | tf_op | source)
XLA Modules:
  0.0 249.5 jit_solution(7094669643221390582)
XLA Ops:
  1.7 1.3 collective-permute-start.1
  3.0 5.5 %collective-permute-start = (bf16[1,64,256]{2,1,0:T(8,128)(2,1)S(1)}, bf16[1,64,256]{2,1,0:T(8,128)(2,1)S(1)}, u32[]{:S(2)}, u32[]{:S(2)}) collective-permute-start(bf16[1,64,256]{2,1,0:T(8,128)(2,1)S(1)} %get-tuple-element.24), channel_id=1, source_target_pairs={{0,4},{4,8},{8,12},{12,16},{16,20},{20,24},{24,28},{1,5},{5,9},{9,... | collective-permute-start | bytes 98312 | tf_op jit(solution)/shard_map/ppermute | solution.py:22
  8.6 3.3 %all-to-all-start = ((s32[4,1,256]{2,1,0:T(1,128)}), s32[4,1,256]{2,1,0:T(1,128)S(1)}, u32[]{:S(2)}, u32[]{:S(2)}) async-start(s32[4,1,256]{2,1,0:T(1,128)} %bitcast.92), calls=%async_computation | async-start | bytes 8192 | tf_op jit(solution)/shard_map/all_to_all | solution.py:102
  12.8 1.3 collective-permute-start.13
  14.1 3.0 %collective-permute-start.12 = (bf16[3,1,128]{2,1,0:T(2,128)(2,1)S(1)}, bf16[3,1,128]{2,1,0:T(2,128)(2,1)S(1)}, u32[]{:S(2)}, u32[]{:S(2)}) collective-permute-start(bf16[3,1,128]{2,1,0:T(2,128)(2,1)S(1)} %get-tuple-element.28), channel_id=1, source_target_pairs={{0,1},{1,2},{2,3},{4,5},{5,6},{6,7},{8,9},{9,10},{10,11},{12,13},{... | collective-permute-start | bytes 2312 | tf_op jit(solution)/shard_map/ppermute | solution.py:22
  18.3 1.3 reduce.4
  24.1 1.3 collective-permute-start.15
  25.4 4.3 %collective-permute-start.14 = (bf16[3,1,128]{2,1,0:T(2,128)(2,1)S(1)}, bf16[3,1,128]{2,1,0:T(2,128)(2,1)S(1)}, u32[]{:S(2)}, u32[]{:S(2)}) collective-permute-start(bf16[3,1,128]{2,1,0:T(2,128)(2,1)S(1)} %get-tuple-element.26), channel_id=1, source_target_pairs={{0,1},{1,2},{2,3},{4,5},{5,6},{6,7},{8,9},{9,10},{10,11},{12,13},{... | collective-permute-start | bytes 2312 | tf_op jit(solution)/shard_map/ppermute | solution.py:22
  30.6 1.3 collective-permute-start.3
  31.9 4.2 %collective-permute-start.2 = (bf16[4,1,256]{2,1,0:T(2,128)(2,1)S(1)}, bf16[4,1,256]{2,1,0:T(2,128)(2,1)S(1)}, u32[]{:S(2)}, u32[]{:S(2)}) collective-permute-start(bf16[4,1,256]{2,1,0:T(2,128)(2,1)S(1)} %get-tuple-element.18), channel_id=1, source_target_pairs={{0,1},{1,2},{2,3},{4,5},{5,6},{6,7},{8,9},{9,10},{10,11},{12,13},{... | collective-permute-start | bytes 6152 | tf_op jit(solution)/shard_map/ppermute | solution.py:22
  36.0 1.1 convolution_subtract_fusion.5
  37.1 1.3 fusion.77
  38.5 1.3 collective-permute-start.5
  39.8 5.4 %collective-permute-start.4 = (bf16[1,64,256]{2,1,0:T(8,128)(2,1)S(1)}, bf16[1,64,256]{2,1,0:T(8,128)(2,1)S(1)}, u32[]{:S(2)}, u32[]{:S(2)}) collective-permute-start(bf16[1,64,256]{2,1,0:T(8,128)(2,1)S(1)} %get-tuple-element.22), channel_id=1, source_target_pairs={{0,4},{4,8},{8,12},{12,16},{16,20},{20,24},{24,28},{1,5},{5,9},{9,... | collective-permute-start | bytes 98312 | tf_op jit(solution)/shard_map/ppermute | solution.py:22
  46.8 1.3 collective-permute-start.7
  48.1 4.1 %collective-permute-start.6 = (bf16[4,1,256]{2,1,0:T(2,128)(2,1)S(1)}, bf16[4,1,256]{2,1,0:T(2,128)(2,1)S(1)}, u32[]{:S(2)}, u32[]{:S(2)}) collective-permute-start(bf16[4,1,256]{2,1,0:T(2,128)(2,1)S(1)} %get-tuple-element.16), channel_id=1, source_target_pairs={{0,1},{1,2},{2,3},{4,5},{5,6},{6,7},{8,9},{9,10},{10,11},{12,13},{... | collective-permute-start | bytes 6152 | tf_op jit(solution)/shard_map/ppermute | solution.py:22
  53.3 1.3 collective-permute-start.9
  54.6 5.2 %collective-permute-start.8 = (bf16[1,64,256]{2,1,0:T(8,128)(2,1)S(1)}, bf16[1,64,256]{2,1,0:T(8,128)(2,1)S(1)}, u32[]{:S(2)}, u32[]{:S(2)}) collective-permute-start(bf16[1,64,256]{2,1,0:T(8,128)(2,1)S(1)} %get-tuple-element.20), channel_id=1, source_target_pairs={{0,4},{4,8},{8,12},{12,16},{16,20},{20,24},{24,28},{1,5},{5,9},{9,... | collective-permute-start | bytes 98312 | tf_op jit(solution)/shard_map/ppermute | solution.py:22
  60.0 1.4 collective-permute-done.8
  61.4 1.3 collective-permute-start.11
  62.7 4.5 %collective-permute-start.10 = (bf16[4,1,256]{2,1,0:T(2,128)(2,1)S(1)}, bf16[4,1,256]{2,1,0:T(2,128)(2,1)S(1)}, u32[]{:S(2)}, u32[]{:S(2)}) collective-permute-start(bf16[4,1,256]{2,1,0:T(2,128)(2,1)S(1)} %get-tuple-element.14), channel_id=1, source_target_pairs={{0,1},{1,2},{2,3},{4,5},{5,6},{6,7},{8,9},{9,10},{10,11},{12,13},{... | collective-permute-start | bytes 6152 | tf_op jit(solution)/shard_map/ppermute | solution.py:22
  69.0 3.9 %gather_fusion = bf16[1024,256]{1,0:T(8,128)(2,1)S(1)} fusion(bf16[128,256]{1,0:T(8,128)(2,1)S(1)} %bitcast.85, s32[1024]{0:T(1024)S(1)} %broadcast_clamp_fusion.1), kind=kCustom, calls=%fused_computation | custom fusion | bytes 1052672 | tf_op jit(solution)/shard_map/jit(_take)/gather | solution.py:89
  73.9 6.5 %all-to-all-start.1 = ((f32[4,3,256]{2,1,0:T(4,128)}), f32[4,3,256]{2,1,0:T(4,128)S(1)}, u32[]{:S(2)}, u32[]{:S(2)}) async-start(f32[4,3,256]{2,1,0:T(4,128)} %fusion.11), calls=%async_computation.1 | async-start | bytes 32768 | tf_op jit(solution)/shard_map/all_to_all | solution.py:101
  80.4 3.8 %all-to-all-done.1 = f32[4,3,256]{2,1,0:T(4,128)S(1)} async-done(((f32[4,3,256]{2,1,0:T(4,128)}), f32[4,3,256]{2,1,0:T(4,128)S(1)}, u32[]{:S(2)}, u32[]{:S(2)}) %all-to-all-start.1) | async-done | bytes 12320 | tf_op jit(solution)/shard_map/all_to_all | solution.py:101
  84.5 8.2 %scatter_custom_fusion = f32[3,8192]{0,1:T(8,128)} fusion(s32[1024]{0:T(1024)S(1)} %bitcast.97, f32[1024,3]{1,0:T(8,128)S(1)} %copy.21, f32[]{:T(128)} %constant.9.clone.1), kind=kCustom, calls=%fused_computation.3 | custom fusion | flops 3072 | bytes 98308 | tf_op jit(solution)/shard_map/scatter-add | solution.py:105
  92.7 2.8 %copy.22 = f32[1,3,8192]{2,1,0:T(4,128)S(1)} copy(f32[1,3,8192]{1,2,0:T(8,128)} %bitcast.87) | data formatting | bytes 196608
  95.5 36.5 %all-gather.1 = f32[8,3,8192]{2,1,0:T(4,128)S(1)} all-gather(f32[1,3,8192]{2,1,0:T(4,128)S(1)} %copy.22), channel_id=2, replica_groups=mesh['slab'=8,'patch'=4] {'slab'}, dimensions={0}, use_global_device_ids=true | all-gather | bytes 884736 | tf_op jit(solution)/shard_map/all_gather | solution.py:10
  132.3 2.7 %copy.27 = f32[3,8192]{0,1:T(8,128)} copy(f32[3,8192]{1,0:T(4,128)S(1)} %reduce_sum.9) | data formatting | bytes 196608
  134.9 2.8 %copy.24 = f32[3,64,128]{2,1,0:T(8,128)S(1)} copy(f32[3,64,128]{0,2,1:T(8,128)} %bitcast.88) | data formatting | bytes 196608 | tf_op jit(solution)/shard_map/reshape | solution.py:107
  137.9 2.6 %copy.25 = f32[3,64,128]{0,2,1:T(8,128)} copy(f32[3,64,128]{2,1,0:T(8,128)S(1)} %fusion.33) | data formatting | bytes 196608 | tf_op jit(solution)/shard_map/add | solution.py:110
  140.6 99.3 %all_gather.11 = f32[3,32768]{0,1:T(8,128)} all-gather(f32[3,8192]{0,1:T(8,128)} %bitcast.86), channel_id=1, replica_groups=mesh['slab'=8,'patch'=4] {'patch'}, dimensions={1}, use_global_device_ids=true | all-gather | bytes 491520 | tf_op jit(solution)/shard_map/all_gather | solution.py:112
  239.9 8.6 %gather_fusion.1 = f32[1024,3]{1,0:T(8,128)S(1)} fusion(f32[3,32768]{0,1:T(8,128)} %all_gather.11, s32[1024]{0:T(1024)S(1)} %broadcast_clamp_fusion), kind=kCustom, calls=%fused_computation.1 | custom fusion | bytes 28672 | tf_op jit(solution)/shard_map/gather | solution.py:113
  (75 shorter events, 15.5 us)
Async XLA Ops:
  0.6 36.5 %copy-start = (bf16[256,256]{1,0:T(8,128)(2,1)S(1)}, bf16[256,256]{1,0:T(8,128)(2,1)}, u32[]{:S(2)}) copy-start(bf16[256,256]{1,0:T(8,128)(2,1)} %param.19) | copy-start | bytes 393220
  0.6 52.3 %copy-start.6 = (f32[2,64]{1,0:T(2,128)S(1)}, f32[2,64]{1,0:T(2,128)}, u32[]{:S(2)}) copy-start(f32[2,64]{1,0:T(2,128)} %param.15) | copy-start | bytes 1540
  0.7 59.1 %copy-start.1 = (bf16[256,256]{1,0:T(8,128)(2,1)S(1)}, bf16[256,256]{1,0:T(8,128)(2,1)}, u32[]{:S(2)}) copy-start(bf16[256,256]{1,0:T(8,128)(2,1)} %param.16) | copy-start | bytes 393220
  0.7 51.5 %copy-start.2 = (bf16[256,256]{1,0:T(8,128)(2,1)S(1)}, bf16[256,256]{1,0:T(8,128)(2,1)}, u32[]{:S(2)}) copy-start(bf16[256,256]{1,0:T(8,128)(2,1)} %param.17) | copy-start | bytes 393220
  0.7 52.3 %copy-start.7 = (f32[2,64,256]{2,1,0:T(8,128)S(1)}, f32[2,64,256]{2,1,0:T(8,128)}, u32[]{:S(2)}) copy-start(f32[2,64,256]{2,1,0:T(8,128)} %param.14) | copy-start | bytes 393220
  0.7 52.3 %copy-start.8 = (bf16[256,256]{1,0:T(8,128)(2,1)S(1)}, bf16[256,256]{1,0:T(8,128)(2,1)}, u32[]{:S(2)}) copy-start(bf16[256,256]{1,0:T(8,128)(2,1)} %param.18) | copy-start | bytes 393220
  1.7 28.8 %collective-permute-start.1 = (bf16[1,64,256]{2,1,0:T(8,128)(2,1)S(1)}, bf16[1,64,256]{2,1,0:T(8,128)(2,1)S(1)}, u32[]{:S(2)}, u32[]{:S(2)}) collective-permute-start(bf16[1,64,256]{2,1,0:T(8,128)(2,1)S(1)} %get-tuple-element.25), channel_id=1, source_target_pairs={{4,0},{8,4},{12,8},{16,12},{20,16},{24,20},{28,24},{5,1},{9,5},{13... | collective-permute-start | bytes 98312 | tf_op jit(solution)/shard_map/ppermute | solution.py:24
  3.0 27.5 %collective-permute-start = (bf16[1,64,256]{2,1,0:T(8,128)(2,1)S(1)}, bf16[1,64,256]{2,1,0:T(8,128)(2,1)S(1)}, u32[]{:S(2)}, u32[]{:S(2)}) collective-permute-start(bf16[1,64,256]{2,1,0:T(8,128)(2,1)S(1)} %get-tuple-element.24), channel_id=1, source_target_pairs={{0,4},{4,8},{8,12},{12,16},{16,20},{20,24},{24,28},{1,5},{5,9},{9,... | collective-permute-start | bytes 98312 | tf_op jit(solution)/shard_map/ppermute | solution.py:22
  8.6 65.3 %all-to-all-start = ((s32[4,1,256]{2,1,0:T(1,128)}), s32[4,1,256]{2,1,0:T(1,128)S(1)}, u32[]{:S(2)}, u32[]{:S(2)}) async-start(s32[4,1,256]{2,1,0:T(1,128)} %bitcast.92), calls=%async_computation | async-start | bytes 8192 | tf_op jit(solution)/shard_map/all_to_all | solution.py:102
  12.8 10.3 %collective-permute-start.13 = (bf16[3,1,128]{2,1,0:T(2,128)(2,1)S(1)}, bf16[3,1,128]{2,1,0:T(2,128)(2,1)S(1)}, u32[]{:S(2)}, u32[]{:S(2)}) collective-permute-start(bf16[3,1,128]{2,1,0:T(2,128)(2,1)S(1)} %get-tuple-element.29), channel_id=1, source_target_pairs={{1,0},{2,1},{3,2},{5,4},{6,5},{7,6},{9,8},{10,9},{11,10},{13,12},{... | collective-permute-start | bytes 2312 | tf_op jit(solution)/shard_map/ppermute | solution.py:24
  14.1 9.0 %collective-permute-start.12 = (bf16[3,1,128]{2,1,0:T(2,128)(2,1)S(1)}, bf16[3,1,128]{2,1,0:T(2,128)(2,1)S(1)}, u32[]{:S(2)}, u32[]{:S(2)}) collective-permute-start(bf16[3,1,128]{2,1,0:T(2,128)(2,1)S(1)} %get-tuple-element.28), channel_id=1, source_target_pairs={{0,1},{1,2},{2,3},{4,5},{5,6},{6,7},{8,9},{9,10},{10,11},{12,13},{... | collective-permute-start | bytes 2312 | tf_op jit(solution)/shard_map/ppermute | solution.py:22
  24.1 5.6 %collective-permute-start.15 = (bf16[3,1,128]{2,1,0:T(2,128)(2,1)S(1)}, bf16[3,1,128]{2,1,0:T(2,128)(2,1)S(1)}, u32[]{:S(2)}, u32[]{:S(2)}) collective-permute-start(bf16[3,1,128]{2,1,0:T(2,128)(2,1)S(1)} %get-tuple-element.27), channel_id=1, source_target_pairs={{1,0},{2,1},{3,2},{5,4},{6,5},{7,6},{9,8},{10,9},{11,10},{13,12},{... | collective-permute-start | bytes 2312 | tf_op jit(solution)/shard_map/ppermute | solution.py:24
  25.4 5.1 %collective-permute-start.14 = (bf16[3,1,128]{2,1,0:T(2,128)(2,1)S(1)}, bf16[3,1,128]{2,1,0:T(2,128)(2,1)S(1)}, u32[]{:S(2)}, u32[]{:S(2)}) collective-permute-start(bf16[3,1,128]{2,1,0:T(2,128)(2,1)S(1)} %get-tuple-element.26), channel_id=1, source_target_pairs={{0,1},{1,2},{2,3},{4,5},{5,6},{6,7},{8,9},{9,10},{10,11},{12,13},{... | collective-permute-start | bytes 2312 | tf_op jit(solution)/shard_map/ppermute | solution.py:22
  30.6 6.6 %collective-permute-start.3 = (bf16[4,1,256]{2,1,0:T(2,128)(2,1)S(1)}, bf16[4,1,256]{2,1,0:T(2,128)(2,1)S(1)}, u32[]{:S(2)}, u32[]{:S(2)}) collective-permute-start(bf16[4,1,256]{2,1,0:T(2,128)(2,1)S(1)} %get-tuple-element.19), channel_id=1, source_target_pairs={{1,0},{2,1},{3,2},{5,4},{6,5},{7,6},{9,8},{10,9},{11,10},{13,12},{... | collective-permute-start | bytes 6152 | tf_op jit(solution)/shard_map/ppermute | solution.py:24
  31.9 5.3 %collective-permute-start.2 = (bf16[4,1,256]{2,1,0:T(2,128)(2,1)S(1)}, bf16[4,1,256]{2,1,0:T(2,128)(2,1)S(1)}, u32[]{:S(2)}, u32[]{:S(2)}) collective-permute-start(bf16[4,1,256]{2,1,0:T(2,128)(2,1)S(1)} %get-tuple-element.18), channel_id=1, source_target_pairs={{0,1},{1,2},{2,3},{4,5},{5,6},{6,7},{8,9},{9,10},{10,11},{12,13},{... | collective-permute-start | bytes 6152 | tf_op jit(solution)/shard_map/ppermute | solution.py:22
  38.5 7.8 %collective-permute-start.5 = (bf16[1,64,256]{2,1,0:T(8,128)(2,1)S(1)}, bf16[1,64,256]{2,1,0:T(8,128)(2,1)S(1)}, u32[]{:S(2)}, u32[]{:S(2)}) collective-permute-start(bf16[1,64,256]{2,1,0:T(8,128)(2,1)S(1)} %get-tuple-element.23), channel_id=1, source_target_pairs={{4,0},{8,4},{12,8},{16,12},{20,16},{24,20},{28,24},{5,1},{9,5},{13... | collective-permute-start | bytes 98312 | tf_op jit(solution)/shard_map/ppermute | solution.py:24
  39.8 7.0 %collective-permute-start.4 = (bf16[1,64,256]{2,1,0:T(8,128)(2,1)S(1)}, bf16[1,64,256]{2,1,0:T(8,128)(2,1)S(1)}, u32[]{:S(2)}, u32[]{:S(2)}) collective-permute-start(bf16[1,64,256]{2,1,0:T(8,128)(2,1)S(1)} %get-tuple-element.22), channel_id=1, source_target_pairs={{0,4},{4,8},{8,12},{12,16},{16,20},{20,24},{24,28},{1,5},{5,9},{9,... | collective-permute-start | bytes 98312 | tf_op jit(solution)/shard_map/ppermute | solution.py:22
  46.8 5.6 %collective-permute-start.7 = (bf16[4,1,256]{2,1,0:T(2,128)(2,1)S(1)}, bf16[4,1,256]{2,1,0:T(2,128)(2,1)S(1)}, u32[]{:S(2)}, u32[]{:S(2)}) collective-permute-start(bf16[4,1,256]{2,1,0:T(2,128)(2,1)S(1)} %get-tuple-element.17), channel_id=1, source_target_pairs={{1,0},{2,1},{3,2},{5,4},{6,5},{7,6},{9,8},{10,9},{11,10},{13,12},{... | collective-permute-start | bytes 6152 | tf_op jit(solution)/shard_map/ppermute | solution.py:24
  48.1 4.9 %collective-permute-start.6 = (bf16[4,1,256]{2,1,0:T(2,128)(2,1)S(1)}, bf16[4,1,256]{2,1,0:T(2,128)(2,1)S(1)}, u32[]{:S(2)}, u32[]{:S(2)}) collective-permute-start(bf16[4,1,256]{2,1,0:T(2,128)(2,1)S(1)} %get-tuple-element.16), channel_id=1, source_target_pairs={{0,1},{1,2},{2,3},{4,5},{5,6},{6,7},{8,9},{9,10},{10,11},{12,13},{... | collective-permute-start | bytes 6152 | tf_op jit(solution)/shard_map/ppermute | solution.py:22
  52.4 20.6 %copy-start.9 = (bf16[3,256]{1,0:T(4,128)(2,1)S(1)}, bf16[3,256]{1,0:T(4,128)(2,1)}, u32[]{:S(2)}) copy-start(bf16[3,256]{1,0:T(4,128)(2,1)} %param.20) | copy-start | bytes 4612
  53.3 6.7 %collective-permute-start.9 = (bf16[1,64,256]{2,1,0:T(8,128)(2,1)S(1)}, bf16[1,64,256]{2,1,0:T(8,128)(2,1)S(1)}, u32[]{:S(2)}, u32[]{:S(2)}) collective-permute-start(bf16[1,64,256]{2,1,0:T(8,128)(2,1)S(1)} %get-tuple-element.21), channel_id=1, source_target_pairs={{4,0},{8,4},{12,8},{16,12},{20,16},{24,20},{28,24},{5,1},{9,5},{13... | collective-permute-start | bytes 98312 | tf_op jit(solution)/shard_map/ppermute | solution.py:24
  54.6 6.8 %collective-permute-start.8 = (bf16[1,64,256]{2,1,0:T(8,128)(2,1)S(1)}, bf16[1,64,256]{2,1,0:T(8,128)(2,1)S(1)}, u32[]{:S(2)}, u32[]{:S(2)}) collective-permute-start(bf16[1,64,256]{2,1,0:T(8,128)(2,1)S(1)} %get-tuple-element.20), channel_id=1, source_target_pairs={{0,4},{4,8},{8,12},{12,16},{16,20},{20,24},{24,28},{1,5},{5,9},{9,... | collective-permute-start | bytes 98312 | tf_op jit(solution)/shard_map/ppermute | solution.py:22
  61.4 6.0 %collective-permute-start.11 = (bf16[4,1,256]{2,1,0:T(2,128)(2,1)S(1)}, bf16[4,1,256]{2,1,0:T(2,128)(2,1)S(1)}, u32[]{:S(2)}, u32[]{:S(2)}) collective-permute-start(bf16[4,1,256]{2,1,0:T(2,128)(2,1)S(1)} %get-tuple-element.15), channel_id=1, source_target_pairs={{1,0},{2,1},{3,2},{5,4},{6,5},{7,6},{9,8},{10,9},{11,10},{13,12},{... | collective-permute-start | bytes 6152 | tf_op jit(solution)/shard_map/ppermute | solution.py:24
  62.7 5.4 %collective-permute-start.10 = (bf16[4,1,256]{2,1,0:T(2,128)(2,1)S(1)}, bf16[4,1,256]{2,1,0:T(2,128)(2,1)S(1)}, u32[]{:S(2)}, u32[]{:S(2)}) collective-permute-start(bf16[4,1,256]{2,1,0:T(2,128)(2,1)S(1)} %get-tuple-element.14), channel_id=1, source_target_pairs={{0,1},{1,2},{2,3},{4,5},{5,6},{6,7},{8,9},{9,10},{10,11},{12,13},{... | collective-permute-start | bytes 6152 | tf_op jit(solution)/shard_map/ppermute | solution.py:22
  73.9 10.4 %all-to-all-start.1 = ((f32[4,3,256]{2,1,0:T(4,128)}), f32[4,3,256]{2,1,0:T(4,128)S(1)}, u32[]{:S(2)}, u32[]{:S(2)}) async-start(f32[4,3,256]{2,1,0:T(4,128)} %fusion.11), calls=%async_computation.1 | async-start | bytes 32768 | tf_op jit(solution)/shard_map/all_to_all | solution.py:101
  132.3 5.5 %copy-start.3 = (f32[3,64,128]{2,1,0:T(8,128)S(1)}, f32[3,64,128]{2,1,0:T(8,128)}, u32[]{:S(2)}) copy-start(f32[3,64,128]{2,1,0:T(8,128)} %param.24) | copy-start | bytes 294916
  132.3 5.5 %copy-start.5 = (f32[64,128]{1,0:T(8,128)S(1)}, f32[64,128]{1,0:T(8,128)}, u32[]{:S(2)}) copy-start(f32[64,128]{1,0:T(8,128)} %param.25) | copy-start | bytes 98308
  137.9 102.0 %copy-start.4 = (f32[3,64,128]{2,1,0:T(8,128)}, f32[3,64,128]{2,1,0:T(8,128)S(1)}, u32[]{:S(2)}) copy-start(f32[3,64,128]{2,1,0:T(8,128)S(1)} %fusion.33) | copy-start | bytes 294916
